TPU v7x, 128 devices: a whole 4x4x4 slice. The times are simulated.
128 devices in a mesh: front: 8 (over z, core), panel: 16 (over x, y).
Axes of the slice: x: 4, y: 4, z: 4, core: 2. Of those that a mesh axis runs over, the one named last changes fastest.
Arguments:
- pivot_columns: float32 [8, 8192, 1024], P('front', 'panel')
- child_rows: bfloat16 [8, 16, 16, 4, 8192], P('front', 'panel'), may hold values from -0.375 to 0.375
- slot_rows: int32 [8, 16, 16, 4], P('front', 'panel'), may hold values from -1 to 511, as said below
- parents: int32 [8], replicated, may hold values from 0 to 7, as said below
- pivot_rhs: float32 [8, 1024, 128], P('front'), may hold values from -6 to 6
- boundary_solution: float32 [8, 8192, 128], P('front', 'panel'), may hold values from -6 to 6
Outputs:
- panel_factor: float32 [8, 8192, 1024], P('front', 'panel')
- update_matrix: bfloat16 [8, 8192, 7168], P('front', 'panel')
- front_solution: float32 [8, 8192, 128], P('front', 'panel')
- child_solution: float32 [8, 16, 16, 4, 128], P('front', 'panel')
Inputs may be any that keep to these rules, and one draw needn't show every extreme that they name: parents[c] is the front of this level into which child front c's rows are added; a front may take several children or none. `slot_rows`: the live slots of each tile of 4 slots come first; the rows that one child front sends to one destination device are distinct; for each child front one destination device receives full tiles from every source device.
All inputs are finite; a program needn't handle non-finite values.
Results may differ from a plain program's by a relative error of at most 0.007.
Values may be sent and summed in bfloat16 or wider, within the bound.
A program may use at most 192 MiB of HBM per device.

v0:
```python
import jax
import jax.numpy as jnp
from jax import lax
from jax.sharding import PartitionSpec as P

K = 512
NSTEP = 2


def spread(shard, axis, root):
    mine = lax.axis_index(axis) == root
    return lax.psum(jnp.where(mine, shard, jnp.zeros_like(shard)), axis)


def outer_rows(mine, piece):
    return lax.dot_general(
        mine, piece, (((1,), (1,)), ((), ())), preferred_element_type=jnp.float32
    )


def scatter_term(slots, rows, local_ids, width):
    onehot = (slots.reshape(-1)[None, :] == local_ids[:, None]).astype(jnp.bfloat16)
    return jnp.dot(onehot, rows.reshape(-1, width), preferred_element_type=jnp.float32)


def on_device(pivot_columns, child_rows, slot_rows, parents, pivot_rhs, boundary_solution):
    highest = lax.Precision.HIGHEST
    panel_index = lax.axis_index("panel")
    front_index = lax.axis_index("front")
    piv_cols = pivot_columns[0]
    row_count = piv_cols.shape[0]
    pivots = piv_cols.shape[1]
    width = child_rows.shape[-1]
    rhs_count = pivot_rhs.shape[-1]
    local_ids = jnp.arange(row_count, dtype=jnp.int32)
    glob_rows = panel_index * row_count + local_ids
    rows_out = child_rows[0, 0]
    slots_out = slot_rows[0, 0]
    routed_rows, routed_slots = (
        lax.all_to_all(rows_out, "panel", split_axis=0, concat_axis=0, tiled=True),
        lax.all_to_all(slots_out, "panel", split_axis=0, concat_axis=0, tiled=True),
    )
    piece_rows = lax.all_gather(routed_rows[None], "front", axis=0, tiled=True)
    piece_slots = lax.all_gather(routed_slots[None], "front", axis=0, tiled=True)
    keeping = parents == front_index

    def add_rows(current):
        kept_slots = jnp.where(keeping[:, None, None], piece_slots, -1)
        return scatter_term(kept_slots, piece_rows, local_ids, width)

    def keep_same(current):
        return current

    assembled = lax.cond(
        jnp.any(keeping), add_rows, keep_same, jnp.zeros((row_count, width), jnp.float32)
    )
    work = assembled + jnp.concatenate(
        [piv_cols, jnp.zeros((row_count, width - pivots), jnp.float32)], axis=1
    )
    identity_block = jnp.eye(K, dtype=jnp.float32)

    def factor_block(values):
        lower = jnp.linalg.cholesky(values)
        return lax.linalg.triangular_solve(lower, identity_block, left_side=True, lower=True)

    def empty_block(values):
        return jnp.zeros_like(values)

    factors = []
    inverses = []
    for panel_step in range(NSTEP):
        low_edge = panel_step * K
        high_edge = low_edge + K
        root_rank = low_edge // row_count
        offset = low_edge - root_rank * row_count
        pivot_block = work[offset : offset + K, low_edge:high_edge]
        inverse = lax.cond(panel_index == root_rank, factor_block, empty_block, pivot_block)
        inverse = spread(inverse, "panel", root_rank)
        column = jnp.dot(work[:, low_edge:high_edge], inverse.T, precision=highest)
        column = jnp.where(glob_rows[:, None] >= low_edge, column, 0.0)
        packed = column.astype(jnp.bfloat16)
        factors.append(column)
        inverses.append(inverse)
        work = work - outer_rows(packed, lax.all_gather(packed, "panel", axis=0, tiled=True))
    factor_all = jnp.concatenate(factors, axis=1)
    trailing = work[:, pivots:]
    update_matrix = jnp.where(glob_rows[:, None] >= pivots, trailing, 0.0).astype(jnp.bfloat16)
    known = boundary_solution[0]
    right_side = pivot_rhs[0]

    def local_values(solved):
        extended = jnp.concatenate([solved, jnp.zeros((row_count, rhs_count), jnp.float32)], axis=0)
        begin = jnp.minimum(panel_index * row_count, pivots)
        segment = lax.dynamic_slice_in_dim(extended, begin, row_count)
        return jnp.where(glob_rows[:, None] < pivots, segment, known)

    solved = jnp.zeros((pivots, rhs_count), jnp.float32)
    contract_rows = (((0,), (0,)), ((), ()))
    for panel_step in reversed(range(NSTEP)):
        low_edge = panel_step * K
        high_edge = low_edge + K
        current = local_values(solved)
        masked = jnp.where(glob_rows[:, None] >= high_edge, factors[panel_step], 0.0)
        partial_sum = lax.dot_general(masked, current, contract_rows, precision=highest)
        carried = lax.psum(partial_sum, "panel")
        value = lax.dot_general(
            inverses[panel_step],
            right_side[low_edge:high_edge] - carried,
            contract_rows,
            precision=highest,
        )
        solved = solved.at[low_edge:high_edge].set(value)
    front_values = local_values(solved)
    slot_onehot = (routed_slots[..., None] == local_ids).astype(jnp.float32)
    piece = lax.all_gather(front_values[None], "front", axis=0, tiled=True)
    piece_count = piece.shape[0]
    weights = (jnp.arange(piece_count, dtype=jnp.int32) == parents[front_index]).astype(jnp.float32)
    chosen = jnp.einsum("n,nrh->rh", weights, piece, precision=highest)
    slot_values = jnp.einsum("psr,rh->psh", slot_onehot, chosen, precision=highest)
    child_values = lax.all_to_all(slot_values, "panel", split_axis=0, concat_axis=0, tiled=True)
    return (factor_all[None], update_matrix[None], front_values[None], child_values[None, None])


def solution(mesh):
    in_specs = (
        P("front", "panel", None),
        P("front", "panel", None, None, None),
        P("front", "panel", None, None),
        P(),
        P("front", None, None),
        P("front", "panel", None),
    )
    out_specs = (
        P("front", "panel", None),
        P("front", "panel", None),
        P("front", "panel", None),
        P("front", "panel", None, None, None),
    )
    return jax.shard_map(
        on_device, mesh=mesh, in_specs=in_specs, out_specs=out_specs, check_vma=False
    )
```

profile of v0, /device:TPU:0, one launch (start us, length us, event | category | flops | bytes accessed | tf_op | source)
XLA Modules:
  0.0 1002.9 jit_solution(4517287727802942974)
XLA Ops:
  7.2 24.1 %all_to_all.19 = bf16[16,4,8192]{2,1,0:T(4,128)(2,1)} all-to-all(bf16[16,4,8192]{2,1,0:T(4,128)(2,1)} %bitcast.145), channel_id=1, replica_groups=mesh['front'=8,'panel'=16] {'panel'}, dimensions={0} | all-to-all | bytes 2097152 | tf_op jit(solution)/shard_map/all_to_all | solution.py:40
  31.3 1.4 copy.30
  32.7 3.8 all-to-all-start
  38.6 5.4 all-to-all-done
  44.0 14.0 %all-gather = s32[128,1,4]{2,1,0:T(1,128)S(1)} all-gather(s32[16,1,4]{2,1,0:T(1,128)S(1)} %all-to-all-done), channel_id=2, replica_groups=mesh['front'=8,'panel'=16] {'front'}, dimensions={0}, use_global_device_ids=true | all-gather | bytes 2304 | tf_op jit(solution)/shard_map/all_gather | solution.py:44
  58.0 22.9 %all-gather.12.cloned.1.call-done = bf16[128,4,8192]{2,1,0:T(4,128)(2,1)} async-done(((bf16[16,4,8192]{2,1,0:T(4,128)(2,1)}), bf16[128,4,8192]{2,1,0:T(4,128)(2,1)}) %all-gather.12.cloned.1.call-update) | async-done | bytes 8388624 | tf_op jit(solution)/shard_map/all_gather | solution.py:43
  80.9 24.2 %conditional.3 = (f32[512,8192]{1,0:T(8,128)}) conditional(s32[]{:T(128)} %convert_element_type.26, () %tuple.36, (pred[8]{0:T(512)(128)(4,1)S(1)}, s32[8,16,4]{2,1,0:T(8,128)S(1)}, s32[512]{0:T(512)S(1)}, bf16[8,16,4,8192]{3,2,1,0:T(4,128)(2,1)}) %tuple.137), branch_computations={%region_1.0_spmd, %region_2.3_spmd} | conditional | flops 4295229952 | bytes 41955344 | solution.py:54
  81.0 12.5 %reshape.120 = bf16[512,8192]{1,0:T(8,128)(2,1)} reshape(bf16[8,16,4,8192]{3,2,1,0:T(4,128)(2,1)} %get-tuple-element.54) | data formatting | bytes 16777216 | tf_op jit(solution)/shard_map/cond/branch_1_fun/reshape | solution.py:23
  93.6 11.5 %fusion = f32[512,8192]{1,0:T(8,128)} fusion(bf16[512,8192]{1,0:T(8,128)(2,1)} %reshape.120, s32[512]{0:T(512)S(1)} %eq.3, s32[512]{0:T(512)S(1)} %get-tuple-element.53), kind=kOutput, calls=%fused_computation | convolution fusion | flops 4295229440 | bytes 25169920 | tf_op jit(solution)/shard_map/cond/branch_1_fun/dot_general | solution.py:23
  105.0 7.0 pad_add_fusion
  112.0 5.7 copy-done
  117.8 141.4 %conditional.4 = (f32[512,512]{0,1:T(8,128)}) conditional(s32[]{:T(128)} %convert_element_type.27, () %tuple.38, (f32[512,512]{1,0:T(8,128)S(1)}, f32[512,512]{1,0:T(8,128)S(1)}) %tuple.39), branch_computations={%region_3.4_spmd, %region_4.15_spmd} | conditional | flops 1412760064 | bytes 26743068 | solution.py:77
  119.7 11.7 %cholesky.286 = f32[128,128]{1,0:T(8,128)S(1)} custom-call(f32[128,128]{1,0:T(8,128)S(1)} %cholesky.426), custom_call_target="Cholesky" | custom-call | tf_op jit(solution)/shard_map/cond/branch_1_fun/jit(cholesky)/cholesky | solution.py:63
  131.4 9.8 custom-call.27
  143.9 11.7 %cholesky.305 = f32[128,128]{1,0:T(8,128)S(1)} custom-call(f32[128,128]{1,0:T(8,128)S(1)} %cholesky.430), custom_call_target="Cholesky" | custom-call | tf_op jit(solution)/shard_map/cond/branch_1_fun/jit(cholesky)/cholesky | solution.py:63
  157.7 10.0 %custom-call.28 = f32[1,128,128]{1,2,0:T(8,128)S(1)} custom-call(f32[1,128,128]{2,1,0:T(8,128)S(1)} %get-tuple-element.139), custom_call_target="InvertDiagBlocksLowerTriangular" | custom-call | tf_op jit(solution)/shard_map/cond/branch_1_fun/jit(cholesky)/cholesky | solution.py:63
  169.3 11.7 %cholesky.326 = f32[128,128]{1,0:T(8,128)S(1)} custom-call(f32[128,128]{1,0:T(8,128)S(1)} %cholesky.435), custom_call_target="Cholesky" | custom-call | tf_op jit(solution)/shard_map/cond/branch_1_fun/jit(cholesky)/cholesky | solution.py:63
  182.3 9.8 custom-call.29
  193.6 11.7 %cholesky.343 = f32[128,128]{1,0:T(8,128)S(1)} custom-call(f32[128,128]{1,0:T(8,128)S(1)} %convolution_subtract_fusion.5), custom_call_target="Cholesky" | custom-call | tf_op jit(solution)/shard_map/cond/branch_1_fun/jit(cholesky)/cholesky | solution.py:63
  207.2 8.0 while.6
  207.9 1.4 bitcast_dynamic-update-slice_fusion.5
  209.9 1.4 bitcast_dynamic-update-slice_fusion.5
  211.9 1.4 bitcast_dynamic-update-slice_fusion.5
  213.9 1.4 bitcast_dynamic-update-slice_fusion.5
  215.3 39.3 %custom-call.30 = f32[4,128,128]{1,2,0:T(8,128)S(1)} custom-call(f32[4,128,128]{2,1,0:T(8,128)S(1)} %get-tuple-element.77), custom_call_target="InvertDiagBlocksLowerTriangular" | custom-call | tf_op jit(solution)/shard_map/cond/branch_1_fun/triangular_solve/custom-call.3 | solution.py:64
  259.3 2.3 broadcast_select_fusion.2
  261.7 82.1 %all-reduce.11.cloned.1.call-done = f32[512,512]{0,1:T(8,128)} async-done(((f32[512,512]{0,1:T(8,128)}), f32[512,512]{0,1:T(8,128)}) %all-reduce.11.cloned.1.call-update) | async-done | bytes 1048592 | tf_op jit(solution)/shard_map/psum | solution.py:12
  343.8 4.2 fusion.110
  348.1 77.5 %all-gather.8.cloned.1.call-done = bf16[8192,512]{0,1:T(8,128)(2,1)} async-done(((bf16[512,512]{0,1:T(8,128)(2,1)}), bf16[8192,512]{0,1:T(8,128)(2,1)}) %all-gather.8.cloned.1.call-update) | async-done | bytes 8388624 | tf_op jit(solution)/shard_map/all_gather | solution.py:84
  425.6 18.7 %convolution_subtract_fusion.12 = f32[512,8192]{1,0:T(8,128)} fusion(f32[512,8192]{1,0:T(8,128)} %copy-done, bf16[512,512]{0,1:T(8,128)(2,1)} %get-tuple-element.163, bf16[8192,512]{0,1:T(8,128)(2,1)} %all-gather.8.cloned.1.call-done), kind=kOutput, calls=%fused_computation.141 | convolution fusion | flops 4299161600 | bytes 42467328 | tf_op jit(solution)/shard_map/dot_general | solution.py:16
  445.6 8.3 conditional.5
  455.1 237.6 %all-reduce.13.cloned.1.call-done = f32[512,512]{0,1:T(8,128)} async-done(((f32[512,512]{0,1:T(8,128)}), f32[512,512]{0,1:T(8,128)}) %all-reduce.13.cloned.1.call-update) | async-done | bytes 1048592 | tf_op jit(solution)/shard_map/psum | solution.py:12
  692.7 4.2 fusion.111
  697.0 1.8 fusion.69
  698.8 83.3 %all-reduce.15.cloned.1.call-done = f32[512,128]{1,0:T(8,128)} async-done(((f32[512,128]{1,0:T(8,128)}), f32[512,128]{1,0:T(8,128)}) %all-reduce.15.cloned.1.call-update) | async-done | bytes 262160 | tf_op jit(solution)/shard_map/psum | solution.py:105
  782.1 2.3 fusion.85
  784.4 1.8 fusion.71
  786.3 83.5 %all-reduce.17.cloned.1.call-done = f32[512,128]{1,0:T(8,128)} async-done(((f32[512,128]{1,0:T(8,128)}), f32[512,128]{1,0:T(8,128)}) %all-reduce.17.cloned.1.call-update) | async-done | bytes 262160 | tf_op jit(solution)/shard_map/psum | solution.py:105
  869.8 2.3 fusion.86
  874.5 23.5 %all-gather.14.cloned.1.call-done = f32[4096,128]{1,0:T(8,128)} async-done(((f32[512,128]{1,0:T(8,128)}), f32[4096,128]{1,0:T(8,128)}) %all-gather.14.cloned.1.call-update) | async-done | bytes 2097168 | tf_op jit(solution)/shard_map/all_gather | solution.py:115
  898.0 4.4 fusion.67
  903.3 7.1 all-to-all-start.2
  910.4 1.5 maximum_bitcast_fusion
  911.9 2.9 copy.37
  914.8 3.1 all-to-all-done.2
  918.0 60.9 %all-gather.10.cloned.1.call-done = bf16[8192,512]{0,1:T(8,128)(2,1)} async-done(((bf16[512,512]{0,1:T(8,128)(2,1)}), bf16[8192,512]{0,1:T(8,128)(2,1)}) %all-gather.10.cloned.1.call-update) | async-done | bytes 8388624 | tf_op jit(solution)/shard_map/all_gather | solution.py:84
  978.8 7.1 fusion.112
  986.0 9.0 fusion.66
  (88 shorter events, 26.3 us)
Async XLA Ops:
  7.2 73.7 %all-gather.12.cloned.1.call-start = ((), (), s32[]{:S(2)}) async-start(), calls=%async_computation.9 | async-start | bytes 9437184 | tf_op jit(solution)/shard_map/all_gather | solution.py:43
  32.7 11.3 %all-to-all-start = ((s32[16,1,4]{2,1,0:T(1,128)}), s32[16,1,4]{2,1,0:T(1,128)S(1)}, u32[]{:S(2)}, u32[]{:S(2)}) async-start(s32[16,1,4]{2,1,0:T(1,128)} %copy.30), calls=%async_computation | async-start | bytes 16384 | tf_op jit(solution)/shard_map/all_to_all | solution.py:41
  36.5 307.3 %all-reduce.11.cloned.1.call-start = ((), (), s32[]{:S(2)}) async-start(), calls=%async_computation.3 | async-start | bytes 2097152 | tf_op jit(solution)/shard_map/psum | solution.py:12
  112.0 5.7 copy-start
  118.7 1.0 copy-start.2
  261.6 164.0 %all-gather.8.cloned.1.call-start = ((), (), s32[]{:S(2)}) async-start(), calls=%async_computation.4 | async-start | bytes 8912896 | tf_op jit(solution)/shard_map/all_gather | solution.py:84
  348.0 344.7 %all-reduce.13.cloned.1.call-start = ((), (), s32[]{:S(2)}) async-start(), calls=%async_computation.5 | async-start | bytes 2097152 | tf_op jit(solution)/shard_map/psum | solution.py:12
  445.6 251.4 %copy-start.4 = (f32[1,512,128]{2,1,0:T(8,128)S(1)}, f32[1,512,128]{2,1,0:T(8,128)}, u32[]{:S(2)}) copy-start(f32[1,512,128]{2,1,0:T(8,128)} %param.24) | copy-start | bytes 786436
  453.8 328.3 %copy-start.6 = (f32[1,1024,128]{2,1,0:T(8,128)S(1)}, f32[1,1024,128]{2,1,0:T(8,128)}, u32[]{:S(2)}) copy-start(f32[1,1024,128]{2,1,0:T(8,128)} %param.23) | copy-start | bytes 1572868
  453.8 419.9 %copy-start.7 = (s32[8]{0:T(128)S(1)}, s32[8]{0:T(128)}, u32[]{:S(2)}) copy-start(s32[8]{0:T(128)} %param.22) | copy-start | bytes 100
  454.9 327.2 %all-reduce.15.cloned.1.call-start = ((), (), s32[]{:S(2)}) async-start(), calls=%async_computation.7 | async-start | bytes 524288 | tf_op jit(solution)/shard_map/psum | solution.py:105
  698.8 171.0 %all-reduce.17.cloned.1.call-start = ((), (), s32[]{:S(2)}) async-start(), calls=%async_computation.8 | async-start | bytes 524288 | tf_op jit(solution)/shard_map/psum | solution.py:105
  784.4 194.4 %copy-start.1 = (bf16[512,512]{0,1:T(8,128)(2,1)S(1)}, bf16[512,512]{0,1:T(8,128)(2,1)}, u32[]{:S(2)}) copy-start(bf16[512,512]{0,1:T(8,128)(2,1)} %get-tuple-element.165) | copy-start | bytes 1572868
  786.2 111.8 %all-gather.14.cloned.1.call-start = ((), (), s32[]{:S(2)}) async-start(), calls=%async_computation.10 | async-start | bytes 2359296 | tf_op jit(solution)/shard_map/all_gather | solution.py:115
  873.0 105.8 %all-gather.10.cloned.1.call-start = ((), (), s32[]{:S(2)}) async-start(), calls=%async_computation.6 | async-start | bytes 8912896 | tf_op jit(solution)/shard_map/all_gather | solution.py:84
  903.3 14.6 %all-to-all-start.2 = ((f32[16,4,128]{2,1,0:T(4,128)}), f32[16,4,128]{2,1,0:T(4,128)S(1)}, u32[]{:S(2)}, u32[]{:S(2)}) async-start(f32[16,4,128]{2,1,0:T(4,128)} %copy.36), calls=%async_computation.2 | async-start | bytes 65536 | tf_op jit(solution)/shard_map/all_to_all | solution.py:120
Sparse Core Ops, SparseCore 0:
  31.4 49.3 all-gather.11
  261.7 82.0 all-reduce.10
  348.1 77.4 all-gather.7
  455.1 237.5 all-reduce.12
  698.9 83.2 all-reduce.14
  786.3 83.3 all-reduce.16
  873.2 24.8 all-gather.13
  900.1 78.6 all-gather.9
where the time goes:
time: 1010 us; the launch traced here: 1000 us
  waiting for transfers between devices  681 us (67%)
  other arithmetic  142 us (14%)
  matrix products  67.1 us (7%)
  blocking collectives  38.1 us (4%)
  local copies, waits for them, and re-layouts  37.7 us (4%)
  between operations  15.5 us (2%)
  starting transfers between devices  11.3 us (1%)
  loops' own time  10.5 us (1%)
    psum x2, waiting for transfers between devices, spread(): return lax.psum(jnp.where(mine, shard, jnp.zeros_like(shard)), axis)  320 us
    psum x2, waiting for transfers between devices, on_device(): carried = lax.psum(partial_sum, 'panel')  167 us
    all_gather x2, waiting for transfers between devices, on_device(): lax.all_gather(packed, 'panel', axis=0, tiled=True)  138 us
    another operation x14, other arithmetic, factor_block(): lower = jnp.linalg.cholesky(values)  78.6 us
    another operation x5, other arithmetic, factor_block(): lax.linalg.triangular_solve(lower, identity_block, left_side=True, lower=...  40 us
    dot_general x2, matrix products, outer_rows(): lax.dot_general(mine, piece, (((1,), (1,)), ((), ())), preferred_element_...  25.8 us
    all_to_all x1, blocking collectives, on_device(): lax.all_to_all(rows_out, 'panel', split_axis=0, concat_axis=0, tiled=True)  24.1 us
    all_gather x1, waiting for transfers between devices, on_device(): piece = lax.all_gather(front_values[None], 'front', axis=0, tiled=True)  23.5 us
  transfers between devices with their start and end apart: 10, of which 10 were waited for; matrix products, arithmetic and copies ran while one was open for 1% of the time, Pallas kernels for 0%

commit v1 on v0

--- a/solution.py
+++ b/solution.py
@@ -112,7 +112,10 @@
         solved = solved.at[low_edge:high_edge].set(value)
     front_values = local_values(solved)
     slot_onehot = (routed_slots[..., None] == local_ids).astype(jnp.float32)
-    piece = lax.all_gather(front_values[None], "front", axis=0, tiled=True)
+    piece = jnp.concatenate(
+        lax.all_to_all(jnp.stack([front_values[None]] * lax.axis_size("front")), "front", 0, 0),
+        axis=0,
+    )
     piece_count = piece.shape[0]
     weights = (jnp.arange(piece_count, dtype=jnp.int32) == parents[front_index]).astype(jnp.float32)
     chosen = jnp.einsum("n,nrh->rh", weights, piece, precision=highest)

time: 1010 us -> 981 us (0.971)
  waiting for transfers between devices: 681 us -> 647 us
    all_gather x2, waiting for transfers between devices: 138 us -> 103 us  [on_device(): lax.all_gather(packed, 'panel', axis=0, tiled=True)]
    all_to_all x0 -> x1, waiting for transfers between devices: none -> 26.6 us  [on_device(): lax.all_to_all(jnp.stack([front_values[None]] * lax.axis_size('front')),...]
    all_gather x1 -> x0, waiting for transfers between devices: 23.5 us -> none  [on_device(): piece = lax.all_gather(front_values[None], 'front', axis=0, tiled=True)]
  transfers between devices with their start and end apart: 10 -> 10, of which waited for: 10 -> 10; matrix products, arithmetic and copies ran while one was open for 1% -> 2% of each run, Pallas kernels for 0% -> 0%
where the time goes in v1:
time: 981 us; the launch traced here: 975 us
  waiting for transfers between devices  647 us (66%)
  other arithmetic  142 us (14%)
  matrix products  67.9 us (7%)
  local copies, waits for them, and re-layouts  39.2 us (4%)
  blocking collectives  38.1 us (4%)
  between operations  15.5 us (2%)
  starting transfers between devices  13.7 us (1%)
  loops' own time  10.6 us (1%)
    psum x2, waiting for transfers between devices, spread(): return lax.psum(jnp.where(mine, shard, jnp.zeros_like(shard)), axis)  320 us
    psum x2, waiting for transfers between devices, on_device(): carried = lax.psum(partial_sum, 'panel')  166 us
    all_gather x2, waiting for transfers between devices, on_device(): lax.all_gather(packed, 'panel', axis=0, tiled=True)  103 us
    another operation x14, other arithmetic, factor_block(): lower = jnp.linalg.cholesky(values)  78.6 us
    another operation x5, other arithmetic, factor_block(): lax.linalg.triangular_solve(lower, identity_block, left_side=True, lower=...  40 us
    all_to_all x1, waiting for transfers between devices, on_device(): lax.all_to_all(jnp.stack([front_values[None]] * lax.axis_size('front')),...  26.6 us
    dot_general x2, matrix products, outer_rows(): lax.dot_general(mine, piece, (((1,), (1,)), ((), ())), preferred_element_...  25.8 us
    all_to_all x1, blocking collectives, on_device(): lax.all_to_all(rows_out, 'panel', split_axis=0, concat_axis=0, tiled=True)  24.1 us
  transfers between devices with their start and end apart: 10, of which 10 were waited for; matrix products, arithmetic and copies ran while one was open for 2% of the time, Pallas kernels for 0%

profile of v1, /device:TPU:0, one launch (start us, length us, event | category | flops | bytes accessed | tf_op | source)
XLA Modules:
  0.0 974.8 jit_solution(18408929871049664572)
XLA Ops:
  7.2 24.1 %all_to_all.24 = bf16[16,4,8192]{2,1,0:T(4,128)(2,1)} all-to-all(bf16[16,4,8192]{2,1,0:T(4,128)(2,1)} %bitcast.144), channel_id=1, replica_groups=mesh['front'=8,'panel'=16] {'panel'}, dimensions={0} | all-to-all | bytes 2097152 | tf_op jit(solution)/shard_map/all_to_all | solution.py:40
  32.7 3.8 all-to-all-start
  38.6 5.4 all-to-all-done
  44.0 14.0 %all-gather = s32[128,1,4]{2,1,0:T(1,128)S(1)} all-gather(s32[16,1,4]{2,1,0:T(1,128)S(1)} %all-to-all-done), channel_id=2, replica_groups=mesh['front'=8,'panel'=16] {'front'}, dimensions={0}, use_global_device_ids=true | all-gather | bytes 2304 | tf_op jit(solution)/shard_map/all_gather | solution.py:44
  58.0 22.9 %all-gather.10.cloned.1.call-done = bf16[128,4,8192]{2,1,0:T(4,128)(2,1)} async-done(((bf16[16,4,8192]{2,1,0:T(4,128)(2,1)}), bf16[128,4,8192]{2,1,0:T(4,128)(2,1)}) %all-gather.10.cloned.1.call-update) | async-done | bytes 8388624 | tf_op jit(solution)/shard_map/all_gather | solution.py:43
  80.9 24.2 %conditional.3 = (f32[512,8192]{1,0:T(8,128)}) conditional(s32[]{:T(128)} %convert_element_type.26, () %tuple.36, (pred[8]{0:T(512)(128)(4,1)S(1)}, s32[8,16,4]{2,1,0:T(8,128)S(1)}, s32[512]{0:T(512)S(1)}, bf16[8,16,4,8192]{3,2,1,0:T(4,128)(2,1)}) %tuple.135), branch_computations={%region_1.0_spmd, %region_2.3_spmd} | conditional | flops 4295229952 | bytes 41955344 | solution.py:54
  81.0 12.5 %reshape.124 = bf16[512,8192]{1,0:T(8,128)(2,1)} reshape(bf16[8,16,4,8192]{3,2,1,0:T(4,128)(2,1)} %get-tuple-element.54) | data formatting | bytes 16777216 | tf_op jit(solution)/shard_map/cond/branch_1_fun/reshape | solution.py:23
  93.6 11.5 %fusion = f32[512,8192]{1,0:T(8,128)} fusion(bf16[512,8192]{1,0:T(8,128)(2,1)} %reshape.124, s32[512]{0:T(512)S(1)} %eq.3, s32[512]{0:T(512)S(1)} %get-tuple-element.53), kind=kOutput, calls=%fused_computation | convolution fusion | flops 4295229440 | bytes 25169920 | tf_op jit(solution)/shard_map/cond/branch_1_fun/dot_general | solution.py:23
  105.0 7.0 pad_add_fusion
  112.0 5.7 copy-done
  117.8 141.4 %conditional.4 = (f32[512,512]{0,1:T(8,128)}) conditional(s32[]{:T(128)} %convert_element_type.27, () %tuple.38, (f32[512,512]{1,0:T(8,128)S(1)}, f32[512,512]{1,0:T(8,128)S(1)}) %tuple.39), branch_computations={%region_3.4_spmd, %region_4.15_spmd} | conditional | flops 1412760064 | bytes 26743068 | solution.py:77
  119.7 11.7 %cholesky.286 = f32[128,128]{1,0:T(8,128)S(1)} custom-call(f32[128,128]{1,0:T(8,128)S(1)} %cholesky.426), custom_call_target="Cholesky" | custom-call | tf_op jit(solution)/shard_map/cond/branch_1_fun/jit(cholesky)/cholesky | solution.py:63
  131.4 9.8 %custom-call.27 = f32[1,128,128]{1,2,0:T(8,128)S(1)} custom-call(f32[1,128,128]{2,1,0:T(8,128)S(1)} %get-tuple-element.142), custom_call_target="InvertDiagBlocksLowerTriangular" | custom-call | tf_op jit(solution)/shard_map/cond/branch_1_fun/jit(cholesky)/cholesky | solution.py:63
  143.9 11.7 %cholesky.305 = f32[128,128]{1,0:T(8,128)S(1)} custom-call(f32[128,128]{1,0:T(8,128)S(1)} %cholesky.430), custom_call_target="Cholesky" | custom-call | tf_op jit(solution)/shard_map/cond/branch_1_fun/jit(cholesky)/cholesky | solution.py:63
  157.7 10.0 %custom-call.28 = f32[1,128,128]{1,2,0:T(8,128)S(1)} custom-call(f32[1,128,128]{2,1,0:T(8,128)S(1)} %get-tuple-element.139), custom_call_target="InvertDiagBlocksLowerTriangular" | custom-call | tf_op jit(solution)/shard_map/cond/branch_1_fun/jit(cholesky)/cholesky | solution.py:63
  169.3 11.7 %cholesky.326 = f32[128,128]{1,0:T(8,128)S(1)} custom-call(f32[128,128]{1,0:T(8,128)S(1)} %cholesky.435), custom_call_target="Cholesky" | custom-call | tf_op jit(solution)/shard_map/cond/branch_1_fun/jit(cholesky)/cholesky | solution.py:63
  182.3 9.8 %custom-call.29 = f32[1,128,128]{1,2,0:T(8,128)S(1)} custom-call(f32[1,128,128]{2,1,0:T(8,128)S(1)} %get-tuple-element.136), custom_call_target="InvertDiagBlocksLowerTriangular" | custom-call | tf_op jit(solution)/shard_map/cond/branch_1_fun/jit(cholesky)/cholesky | solution.py:63
  193.6 11.7 %cholesky.343 = f32[128,128]{1,0:T(8,128)S(1)} custom-call(f32[128,128]{1,0:T(8,128)S(1)} %convolution_subtract_fusion.5), custom_call_target="Cholesky" | custom-call | tf_op jit(solution)/shard_map/cond/branch_1_fun/jit(cholesky)/cholesky | solution.py:63
  207.2 8.0 while.6
  207.9 1.4 bitcast_dynamic-update-slice_fusion.5
  209.9 1.4 bitcast_dynamic-update-slice_fusion.5
  211.9 1.4 bitcast_dynamic-update-slice_fusion.5
  215.3 39.3 %custom-call.30 = f32[4,128,128]{1,2,0:T(8,128)S(1)} custom-call(f32[4,128,128]{2,1,0:T(8,128)S(1)} %get-tuple-element.77), custom_call_target="InvertDiagBlocksLowerTriangular" | custom-call | tf_op jit(solution)/shard_map/cond/branch_1_fun/triangular_solve/custom-call.3 | solution.py:64
  259.3 2.3 broadcast_select_fusion.2
  261.7 82.1 %all-reduce.11.cloned.1.call-done = f32[512,512]{0,1:T(8,128)} async-done(((f32[512,512]{0,1:T(8,128)}), f32[512,512]{0,1:T(8,128)}) %all-reduce.11.cloned.1.call-update) | async-done | bytes 1048592 | tf_op jit(solution)/shard_map/psum | solution.py:12
  343.8 4.2 fusion.110
  348.1 77.5 %all-gather.6.cloned.1.call-done = bf16[8192,512]{0,1:T(8,128)(2,1)} async-done(((bf16[512,512]{0,1:T(8,128)(2,1)}), bf16[8192,512]{0,1:T(8,128)(2,1)}) %all-gather.6.cloned.1.call-update) | async-done | bytes 8388624 | tf_op jit(solution)/shard_map/all_gather | solution.py:84
  425.6 18.7 %convolution_subtract_fusion.12 = f32[512,8192]{1,0:T(8,128)} fusion(f32[512,8192]{1,0:T(8,128)} %copy-done, bf16[512,512]{0,1:T(8,128)(2,1)} %get-tuple-element.163, bf16[8192,512]{0,1:T(8,128)(2,1)} %all-gather.6.cloned.1.call-done), kind=kOutput, calls=%fused_computation.141 | convolution fusion | flops 4299161600 | bytes 42467328 | tf_op jit(solution)/shard_map/dot_general | solution.py:16
  445.6 8.4 conditional.5
  455.3 237.5 %all-reduce.13.cloned.1.call-done = f32[512,512]{0,1:T(8,128)} async-done(((f32[512,512]{0,1:T(8,128)}), f32[512,512]{0,1:T(8,128)}) %all-reduce.13.cloned.1.call-update) | async-done | bytes 1048592 | tf_op jit(solution)/shard_map/psum | solution.py:12
  692.7 4.2 fusion.111
  697.0 1.8 fusion.69
  698.9 83.3 %all-reduce.15.cloned.1.call-done = f32[512,128]{1,0:T(8,128)} async-done(((f32[512,128]{1,0:T(8,128)}), f32[512,128]{1,0:T(8,128)}) %all-reduce.15.cloned.1.call-update) | async-done | bytes 262160 | tf_op jit(solution)/shard_map/psum | solution.py:105
  782.2 2.3 fusion.85
  784.5 2.7 fusion.71
  788.0 82.8 %all-reduce.17.cloned.1.call-done = f32[512,128]{1,0:T(8,128)} async-done(((f32[512,128]{1,0:T(8,128)}), f32[512,128]{1,0:T(8,128)}) %all-reduce.17.cloned.1.call-update) | async-done | bytes 262160 | tf_op jit(solution)/shard_map/psum | solution.py:105
  870.8 2.0 fusion.86
  874.0 1.5 stack.3
  875.4 4.4 all-to-all-start.2
  880.6 26.6 %all-to-all-done.2 = f32[8,1,512,128]{3,2,1,0:T(8,128)} async-done(((f32[8,1,512,128]{3,2,1,0:T(8,128)}), f32[8,1,512,128]{3,2,1,0:T(8,128)}, u32[]{:S(2)}, u32[]{:S(2)}) %all-to-all-start.2) | async-done | bytes 2097184 | tf_op jit(solution)/shard_map/all_to_all | solution.py:116
  907.2 4.5 fusion.67
  912.6 5.2 all-to-all-start.3
  917.8 1.5 maximum_bitcast_fusion
  919.3 2.9 copy.37
  922.1 3.2 all-to-all-done.3
  925.3 25.4 %all-gather.8.cloned.1.call-done = bf16[8192,512]{0,1:T(8,128)(2,1)} async-done(((bf16[512,512]{0,1:T(8,128)(2,1)}), bf16[8192,512]{0,1:T(8,128)(2,1)}) %all-gather.8.cloned.1.call-update) | async-done | bytes 8388624 | tf_op jit(solution)/shard_map/all_gather | solution.py:84
  950.7 7.1 fusion.112
  957.9 9.0 fusion.66
  (90 shorter events, 29.2 us)
Async XLA Ops:
  7.2 73.7 %all-gather.10.cloned.1.call-start = ((), (), s32[]{:S(2)}) async-start(), calls=%async_computation.10 | async-start | bytes 9437184 | tf_op jit(solution)/shard_map/all_gather | solution.py:43
  32.7 11.3 %all-to-all-start = ((s32[16,1,4]{2,1,0:T(1,128)}), s32[16,1,4]{2,1,0:T(1,128)S(1)}, u32[]{:S(2)}, u32[]{:S(2)}) async-start(s32[16,1,4]{2,1,0:T(1,128)} %copy.30), calls=%async_computation | async-start | bytes 16384 | tf_op jit(solution)/shard_map/all_to_all | solution.py:41
  36.5 307.3 %all-reduce.11.cloned.1.call-start = ((), (), s32[]{:S(2)}) async-start(), calls=%async_computation.4 | async-start | bytes 2097152 | tf_op jit(solution)/shard_map/psum | solution.py:12
  112.0 5.7 copy-start
  118.7 1.0 copy-start.3
  261.6 164.0 %all-gather.6.cloned.1.call-start = ((), (), s32[]{:S(2)}) async-start(), calls=%async_computation.5 | async-start | bytes 8912896 | tf_op jit(solution)/shard_map/all_gather | solution.py:84
  348.0 344.7 %all-reduce.13.cloned.1.call-start = ((), (), s32[]{:S(2)}) async-start(), calls=%async_computation.6 | async-start | bytes 2097152 | tf_op jit(solution)/shard_map/psum | solution.py:12
  445.6 251.4 %copy-start.5 = (f32[1,512,128]{2,1,0:T(8,128)S(1)}, f32[1,512,128]{2,1,0:T(8,128)}, u32[]{:S(2)}) copy-start(f32[1,512,128]{2,1,0:T(8,128)} %param.24) | copy-start | bytes 786436
  454.0 416.8 %copy-start.2 = (f32[512,512]{0,1:T(8,128)S(1)}, f32[512,512]{0,1:T(8,128)}, u32[]{:S(2)}) copy-start(f32[512,512]{0,1:T(8,128)} %all-reduce.11.cloned.1.call-done) | copy-start | bytes 3145732
  455.1 327.1 %all-reduce.15.cloned.1.call-start = ((), (), s32[]{:S(2)}) async-start(), calls=%async_computation.8 | async-start | bytes 524288 | tf_op jit(solution)/shard_map/psum | solution.py:105
  697.0 182.9 %copy-start.8 = (s32[8]{0:T(128)S(1)}, s32[8]{0:T(128)}, u32[]{:S(2)}) copy-start(s32[8]{0:T(128)} %param.22) | copy-start | bytes 100
  698.8 172.0 %all-reduce.17.cloned.1.call-start = ((), (), s32[]{:S(2)}) async-start(), calls=%async_computation.9 | async-start | bytes 524288 | tf_op jit(solution)/shard_map/psum | solution.py:105
  787.3 163.5 %all-gather.8.cloned.1.call-start = ((), (), s32[]{:S(2)}) async-start(), calls=%async_computation.7 | async-start | bytes 8912896 | tf_op jit(solution)/shard_map/all_gather | solution.py:84
  874.0 48.2 %copy-start.6 = (f32[512,128]{1,0:T(8,128)}, f32[512,128]{1,0:T(8,128)S(1)}, u32[]{:S(2)}) copy-start(f32[512,128]{1,0:T(8,128)S(1)} %fusion.82) | copy-start | bytes 786436
  874.0 76.8 %copy-start.1 = (bf16[512,512]{0,1:T(8,128)(2,1)S(1)}, bf16[512,512]{0,1:T(8,128)(2,1)}, u32[]{:S(2)}) copy-start(bf16[512,512]{0,1:T(8,128)(2,1)} %get-tuple-element.165) | copy-start | bytes 1572868
  875.4 31.7 %all-to-all-start.2 = ((f32[8,1,512,128]{3,2,1,0:T(8,128)}), f32[8,1,512,128]{3,2,1,0:T(8,128)}, u32[]{:S(2)}, u32[]{:S(2)}) async-start(f32[8,1,512,128]{3,2,1,0:T(8,128)} %stack.3), calls=%async_computation.2 | async-start | bytes 4194304 | tf_op jit(solution)/shard_map/all_to_all | solution.py:116
  912.6 12.7 %all-to-all-start.3 = ((f32[16,4,128]{2,1,0:T(4,128)}), f32[16,4,128]{2,1,0:T(4,128)S(1)}, u32[]{:S(2)}, u32[]{:S(2)}) async-start(f32[16,4,128]{2,1,0:T(4,128)} %copy.36), calls=%async_computation.3 | async-start | bytes 65536 | tf_op jit(solution)/shard_map/all_to_all | solution.py:123
Sparse Core Ops, SparseCore 0:
  31.4 49.3 all-gather.9
  261.7 82.0 all-reduce.10
  348.1 77.4 all-gather.5
  455.2 237.5 all-reduce.12
  698.9 83.2 all-reduce.14
  787.4 83.3 all-reduce.16
  872.9 77.8 all-gather.7
